TPU v7x, 32 devices: a whole 2x2x4 slice. The times are simulated.
32 devices in a mesh: sn: 8 (over y, x, core), blk: 4 (over z).
Axes of the slice: x: 2, y: 2, z: 4, core: 2. Of those that a mesh axis runs over, the one named last changes fastest.
Arguments:
- root_inverse: float32 [2048, 2048], P('sn'), as said below
- structure: int32 [8, 4], replicated, may hold values from 0 to 7, as said below
- panel_one: float32 [8, 1024, 256], P('sn', 'blk'), may hold values from -0.375 to 0.375
- inverse_one: float32 [8, 256, 256], P('sn'), as said below
- parent_two: float32 [8, 256, 256], P('sn'), may hold values from -0.375 to 0.375
- panel_two: float32 [8, 1024, 256], P('sn', 'blk'), may hold values from -0.375 to 0.375
- inverse_two: float32 [8, 256, 256], P('sn'), as said below
Outputs:
- sigma_diag_one: float32 [8, 256, 256], P('sn')
- sigma_off_one: float32 [8, 1024, 256], P('sn', 'blk')
- sigma_diag_two: float32 [8, 256, 256], P('sn')
- sigma_par_two: float32 [8, 256, 256], P('sn')
- sigma_root_two: float32 [8, 1024, 256], P('sn', 'blk')
Inputs may be any that keep to these rules, and one draw needn't show every extreme that they name: `structure`: each row holds 4 distinct block indices. `inverse_one`: lower triangular; diagonal between 0.5 and 1.5. `inverse_two`: lower triangular; diagonal between 0.5 and 1.5. `root_inverse`: Symmetric.
All inputs are finite; a program needn't handle non-finite values.
Results may differ from a plain program's by a relative error of at most 0.00011.
Values sent between devices are 32-bit elements; how exact they have to be, the bound alone decides.
No kernel may reach another device: no remote copies, remote signals or barrier semaphores. Data moves between devices by JAX's collectives and lax.ppermute only.
A program may use at most 128 MiB of HBM per device.

v0:
```python
import jax
import jax.numpy as jnp
from jax import lax
from jax.sharding import PartitionSpec as P


def product(left, right):
    return jnp.dot(left, right, precision=lax.Precision.HIGHEST, preferred_element_type=jnp.float32)


def per_device(root_inverse, structure, panel_one, inverse_one, parent_two, panel_two, inverse_two):
    width = inverse_one.shape[-1]
    groups = lax.axis_size("blk")
    per_group = structure.shape[1] // groups
    owner = lax.axis_index("sn")
    position_group = lax.axis_index("blk")
    inv_one = inverse_one[0]
    inv_two = inverse_two[0]
    u_one = product(panel_one[0], inv_one)
    u_root = product(panel_two[0], inv_two)
    u_par = product(parent_two[0], inv_two)
    stacked = jnp.concatenate([u_one, u_root], axis=1)
    group_lists = lax.dynamic_slice_in_dim(structure, position_group * per_group, per_group, 1)
    block_count = root_inverse.shape[1] // width
    local_rows = root_inverse.reshape(root_inverse.shape[0], block_count, width)
    listed_cols = jnp.take(local_rows, structure, axis=1)
    listed_cols = listed_cols.reshape(
        local_rows.shape[0], structure.shape[0], structure.shape[1] * width
    )
    listed_cols = jnp.transpose(listed_cols, (1, 0, 2))
    named = (group_lists == owner).astype(jnp.float32)
    outgoing = named[:, :, None, None] * listed_cols[:, None, :, :]
    incoming = lax.all_to_all(outgoing, "sn", split_axis=0, concat_axis=0, tiled=True)
    own_rows = jnp.sum(incoming, axis=0).reshape(per_group * width, structure.shape[1] * width)
    full_panels = lax.all_gather(stacked, "blk", axis=0, tiled=True)
    combined = product(own_rows, full_panels)
    w_one = combined[:, :width]
    w_two = combined[:, width:]
    off_one = -w_one
    square_one = product(inv_one.T, inv_one)
    square_two = product(inv_two.T, inv_two)
    diag_term = product(u_one.T, w_one)
    root_two = -(w_two + product(off_one, u_par))
    child_term = product(u_root.T, root_two)
    diag_one = square_one + lax.psum(diag_term, "blk")
    parent_total, child_total = lax.psum((product(off_one.T, u_root), child_term), "blk")
    par_two = -(parent_total + product(diag_one, u_par))
    diag_two = square_two - product(u_par.T, par_two) - child_total
    return (diag_one[None], off_one[None], diag_two[None], par_two[None], root_two[None])


def solution(mesh):
    return jax.shard_map(
        per_device,
        mesh=mesh,
        in_specs=(
            P("sn", None),
            P(),
            P("sn", "blk", None),
            P("sn", None, None),
            P("sn", None, None),
            P("sn", "blk", None),
            P("sn", None, None),
        ),
        out_specs=(
            P("sn", None, None),
            P("sn", "blk", None),
            P("sn", None, None),
            P("sn", None, None),
            P("sn", "blk", None),
        ),
        check_vma=False,
    )
```

profile of v0, /device:TPU:0, one launch (start us, length us, event | category | flops | bytes accessed | tf_op | source)
XLA Modules:
  0.0 204.8 jit_solution(13430769693259133787)
XLA Ops:
  7.2 0.7 compare_select_fusion
  7.9 0.7 compare_and_fusion
  8.6 2.9 %copy.18 = f32[256,2048]{0,1:T(8,128)} copy(f32[256,2048]{1,0:T(8,128)} %param.7) | data formatting | bytes 4194304 | tf_op args[0]
  11.5 1.9 copy.20
  13.4 0.1 copy.19
  13.5 0.1 reshape.33
  13.6 4.3 %gather_fusion = f32[32,256,256]{2,1,0:T(8,128)} fusion(f32[256,8,256]{2,0,1:T(8,128)S(1)} %copy.20, s32[1024]{0:T(1024)S(1)} %pad_clamp_fusion), kind=kCustom, calls=%fused_computation | custom fusion | bytes 16777344 | tf_op jit(solution)/shard_map/jit(_take)/gather | solution.py:26
  17.9 9.2 %copy.21 = f32[8,4,256,256]{2,3,1,0:T(8,128)} copy(f32[8,4,256,256]{3,2,1,0:T(8,128)} %bitcast.57) | data formatting | bytes 16777216 | tf_op jit(solution)/shard_map/jit(_take)/gather | solution.py:26
  27.1 0.7 fusion.21
  27.8 0.1 broadcast_in_dim.33
  27.8 7.4 %fusion = f32[256,8,1024]{0,2,1:T(8,128)} fusion(f32[8,4,256,256]{2,3,1,0:T(8,128)} %copy.21, f32[8]{0:T(128)S(1)} %fusion.21, pred[8,1024]{1,0:T(8,128)(4,1)S(1)} %bitcast.63), kind=kLoop, calls=%fused_computation.2 | loop fusion | flops 4194304 | bytes 16785440 | tf_op jit(solution)/shard_map/mul | solution.py:32
  35.3 5.3 %all-to-all-start = ((f32[8,1,256,1024]{2,3,1,0:T(8,128)}), f32[8,1,256,1024]{2,3,1,0:T(8,128)}, u32[]{:S(2)}, u32[]{:S(2)}) async-start(f32[8,1,256,1024]{2,3,1,0:T(8,128)} %bitcast.58), calls=%async_computation | async-start | bytes 16777216 | tf_op jit(solution)/shard_map/all_to_all | solution.py:33
  40.6 0.0 all-gather.2.cloned.1.call-start
  40.7 0.6 fusion.10
  41.3 0.6 fusion.13
  41.9 0.8 pad_maximum_fusion
  42.8 0.2 all-reduce.3.cloned.1.call-start
  43.0 0.4 fusion.5
  43.4 91.7 %all-to-all-done = f32[8,1,256,1024]{2,3,1,0:T(8,128)} async-done(((f32[8,1,256,1024]{2,3,1,0:T(8,128)}), f32[8,1,256,1024]{2,3,1,0:T(8,128)}, u32[]{:S(2)}, u32[]{:S(2)}) %all-to-all-start) | async-done | bytes 8388640 | tf_op jit(solution)/shard_map/all_to_all | solution.py:33
  135.1 4.1 %bitcast_reduce_fusion = f32[256,1024]{0,1:T(8,128)S(1)} fusion(f32[8,1,256,1024]{2,3,1,0:T(8,128)} %all-to-all-done), kind=kLoop, calls=%fused_computation.3 | loop fusion | flops 1835008 | bytes 9437184 | tf_op jit(solution)/shard_map/reduce_sum | solution.py:34
  139.2 0.0 all-gather.2.cloned.1.call-done
  139.2 5.1 %fusion.22 = f32[256,512]{1,0:T(8,128)S(1)} fusion(f32[256,1024]{0,1:T(8,128)S(1)} %bitcast_reduce_fusion, f32[1024,512]{0,1:T(8,128)} %all-gather.2.cloned.1.call-done), kind=kOutput, calls=%fused_computation.35 | convolution fusion | flops 1610612736 | bytes 3670016 | tf_op jit(solution)/shard_map/dot_general | solution.py:8
  144.3 1.3 fusion.19
  145.6 1.1 fusion.17
  146.7 0.4 fusion.1
  147.1 1.1 fusion.23
  148.2 0.6 fusion.8
  148.8 0.7 fusion.20
  149.6 43.0 %all-reduce.3.cloned.1.call-done = (f32[256,256]{1,0:T(8,128)}, f32[256,256]{1,0:T(8,128)}, f32[256,256]{1,0:T(8,128)}) async-done(((f32[256,256]{1,0:T(8,128)}, f32[256,256]{1,0:T(8,128)}, f32[256,256]{1,0:T(8,128)}), (f32[256,256]{1,0:T(8,128)}, f32[256,256]{1,0:T(8,128)}, f32[256,256]{1,0:T(8,128)})) %all-reduce.3.cloned.1.call-update) | async-done | bytes 786448 | tf_op jit(solution)/shard_map/psum | solution.py:45
  192.6 1.5 convolution_add_fusion.2
  194.2 1.4 fusion.4
  195.6 2.4 %fusion.3 = f32[1,256,256]{2,1,0:T(8,128)} fusion(f32[256,256]{1,0:T(8,128)} %get-tuple-element.6, f32[256,256]{1,0:T(8,128)S(1)} %fusion.8, f32[256,256]{1,0:T(8,128)S(1)} %fusion.5, f32[256,256]{1,0:T(8,128)S(1)} %fusion.4), kind=kOutput, calls=%fused_computation.8 | convolution fusion | flops 201457664 | bytes 1310720 | tf_op jit(solution)/shard_map/dot_general | solution.py:8
  (19 shorter events, 0.1 us)
Async XLA Ops:
  7.2 33.5 %copy-start = (f32[1,256,256]{2,1,0:T(8,128)S(1)}, f32[1,256,256]{2,1,0:T(8,128)}, u32[]{:S(2)}) copy-start(f32[1,256,256]{2,1,0:T(8,128)} %param.13) | copy-start | bytes 786436
  35.3 5.4 %copy-start.5 = (f32[1,256,256]{2,1,0:T(8,128)S(1)}, f32[1,256,256]{2,1,0:T(8,128)}, u32[]{:S(2)}) copy-start(f32[1,256,256]{2,1,0:T(8,128)} %param.12) | copy-start | bytes 786436
  35.3 6.0 %copy-start.1 = (f32[1,256,256]{2,1,0:T(8,128)S(1)}, f32[1,256,256]{2,1,0:T(8,128)}, u32[]{:S(2)}) copy-start(f32[1,256,256]{2,1,0:T(8,128)} %param.10) | copy-start | bytes 786436
  35.3 6.0 %copy-start.6 = (f32[1,256,256]{2,1,0:T(8,128)S(1)}, f32[1,256,256]{2,1,0:T(8,128)}, u32[]{:S(2)}) copy-start(f32[1,256,256]{2,1,0:T(8,128)} %param.9) | copy-start | bytes 786436
  35.3 7.7 %copy-start.7 = (f32[1,256,256]{2,1,0:T(8,128)S(1)}, f32[1,256,256]{2,1,0:T(8,128)}, u32[]{:S(2)}) copy-start(f32[1,256,256]{2,1,0:T(8,128)} %param.11) | copy-start | bytes 786436
  35.3 99.8 %all-to-all-start = ((f32[8,1,256,1024]{2,3,1,0:T(8,128)}), f32[8,1,256,1024]{2,3,1,0:T(8,128)}, u32[]{:S(2)}, u32[]{:S(2)}) async-start(f32[8,1,256,1024]{2,3,1,0:T(8,128)} %bitcast.58), calls=%async_computation | async-start | bytes 16777216 | tf_op jit(solution)/shard_map/all_to_all | solution.py:33
  40.6 98.6 %all-gather.2.cloned.1.call-start = ((), (), s32[]{:S(2)}) async-start(), calls=%async_computation.1 | async-start | bytes 2621440 | tf_op jit(solution)/shard_map/all_gather | solution.py:35
  42.8 149.8 %all-reduce.3.cloned.1.call-start = ((), (), s32[]{:S(2)}) async-start(), calls=%async_computation.2 | async-start | bytes 1572864 | tf_op jit(solution)/shard_map/psum | solution.py:45
  147.1 50.8 %copy-start.2 = (f32[256,256]{1,0:T(8,128)}, f32[256,256]{1,0:T(8,128)S(1)}, u32[]{:S(2)}) copy-start(f32[256,256]{1,0:T(8,128)S(1)} %fusion.1) | copy-start | bytes 786436
  194.1 3.8 %copy-start.3 = (f32[256,256]{1,0:T(8,128)}, f32[256,256]{1,0:T(8,128)S(1)}, u32[]{:S(2)}) copy-start(f32[256,256]{1,0:T(8,128)S(1)} %convolution_add_fusion.2) | copy-start | bytes 786436
  195.6 2.4 %copy-start.4 = (f32[256,256]{1,0:T(8,128)}, f32[256,256]{1,0:T(8,128)S(1)}, u32[]{:S(2)}) copy-start(f32[256,256]{1,0:T(8,128)S(1)} %fusion.4) | copy-start | bytes 786436
Sparse Core Ops, SparseCore 0:
  43.0 48.5 all-gather.1
  148.3 44.1 all-reduce.2
where the time goes:
time: 205 us
  waiting for transfers between devices  135 us (66%)
  local copies, waits for them, and re-layouts  18.6 us (9%)
  matrix products  16.4 us (8%)
  other arithmetic  15.2 us (7%)
  between operations  14.2 us (7%)
  starting transfers between devices  5.6 us (3%)
    all_to_all x1, waiting for transfers between devices, per_device(): lax.all_to_all(outgoing, 'sn', split_axis=0, concat_axis=0, tiled=True)  91.7 us
    psum x1, waiting for transfers between devices, per_device(): diag_one = square_one + lax.psum(diag_term, 'blk')  43 us
    dot_general x12, matrix products, product(): jnp.dot(left, right, precision=lax.Precision.HIGHEST, preferred_element_t...  16.4 us
    gather x2, local copies, waits for them, and re-layouts, per_device(): listed_cols = jnp.take(local_rows, structure, axis=1)  13.5 us
    mul x2, other arithmetic, per_device(): outgoing = named[:, :, None, None] * listed_cols[:, None, :, :]  8.12 us
    all_to_all x1, starting transfers between devices, per_device(): lax.all_to_all(outgoing, 'sn', split_axis=0, concat_axis=0, tiled=True)  5.34 us
  transfers between devices with their start and end apart: 3, of which 2 were waited for; matrix products, arithmetic and copies ran while one was open for 4% of the time, Pallas kernels for 0%

commit v1 on v0

--- a/solution.py
+++ b/solution.py
@@ -42,7 +42,7 @@
     diag_term = product(u_one.T, w_one)
     root_two = -(w_two + product(off_one, u_par))
     child_term = product(u_root.T, root_two)
-    diag_one = square_one + lax.psum(diag_term, "blk")
+    diag_one = square_one + jnp.sum(lax.all_gather(diag_term, "blk"), axis=0)
     parent_total, child_total = lax.psum((product(off_one.T, u_root), child_term), "blk")
     par_two = -(parent_total + product(diag_one, u_par))
     diag_two = square_two - product(u_par.T, par_two) - child_total

time: 205 us -> 226 us (1.10)
  waiting for transfers between devices: 135 us -> 155 us
    all_gather x0 -> x1, waiting for transfers between devices: none -> 23.6 us  [per_device(): diag_one = square_one + jnp.sum(lax.all_gather(diag_term, 'blk'), axis=0)]
    psum x1, waiting for transfers between devices: 43 us -> 39.1 us  [per_device(): lax.psum((product(off_one.T, u_root), child_term), 'blk')]
  transfers between devices with their start and end apart: 3 -> 4, of which waited for: 2 -> 3; matrix products, arithmetic and copies ran while one was open for 4% -> 6% of each run, Pallas kernels for 0% -> 0%
where the time goes in v1:
time: 226 us; the launch traced here: 225 us
  waiting for transfers between devices  155 us (69%)
  local copies, waits for them, and re-layouts  18.6 us (8%)
  other arithmetic  16.5 us (7%)
  matrix products  15.4 us (7%)
  between operations  13.9 us (6%)
  starting transfers between devices  5.64 us (2%)
    all_to_all x1, waiting for transfers between devices, per_device(): lax.all_to_all(outgoing, 'sn', split_axis=0, concat_axis=0, tiled=True)  92.3 us
    psum x1, waiting for transfers between devices, per_device(): lax.psum((product(off_one.T, u_root), child_term), 'blk')  39.1 us
    all_gather x1, waiting for transfers between devices, per_device(): diag_one = square_one + jnp.sum(lax.all_gather(diag_term, 'blk'), axis=0)  23.6 us
    dot_general x12, matrix products, product(): jnp.dot(left, right, precision=lax.Precision.HIGHEST, preferred_element_t...  15.4 us
    gather x2, local copies, waits for them, and re-layouts, per_device(): listed_cols = jnp.take(local_rows, structure, axis=1)  13.5 us
    mul x2, other arithmetic, per_device(): outgoing = named[:, :, None, None] * listed_cols[:, None, :, :]  8.12 us
    all_to_all x1, starting transfers between devices, per_device(): lax.all_to_all(outgoing, 'sn', split_axis=0, concat_axis=0, tiled=True)  5.34 us
  transfers between devices with their start and end apart: 4, of which 3 were waited for; matrix products, arithmetic and copies ran while one was open for 6% of the time, Pallas kernels for 0%

profile of v1, /device:TPU:0, one launch (start us, length us, event | category | flops | bytes accessed | tf_op | source)
XLA Modules:
  0.0 225.1 jit_solution(2383565569119919262)
XLA Ops:
  7.2 0.7 compare_select_fusion
  7.9 0.7 compare_and_fusion
  8.6 2.9 %copy.18 = f32[256,2048]{0,1:T(8,128)} copy(f32[256,2048]{1,0:T(8,128)} %param.7) | data formatting | bytes 4194304 | tf_op args[0]
  11.5 1.9 copy.20
  13.4 0.1 copy.19
  13.5 0.1 reshape.33
  13.6 4.3 %gather_fusion = f32[32,256,256]{2,1,0:T(8,128)} fusion(f32[256,8,256]{2,0,1:T(8,128)S(1)} %copy.20, s32[1024]{0:T(1024)S(1)} %pad_clamp_fusion), kind=kCustom, calls=%fused_computation | custom fusion | bytes 16777344 | tf_op jit(solution)/shard_map/jit(_take)/gather | solution.py:26
  17.9 9.2 %copy.21 = f32[8,4,256,256]{2,3,1,0:T(8,128)} copy(f32[8,4,256,256]{3,2,1,0:T(8,128)} %bitcast.58) | data formatting | bytes 16777216 | tf_op jit(solution)/shard_map/jit(_take)/gather | solution.py:26
  27.1 0.7 fusion.21
  27.8 0.1 broadcast_in_dim.33
  27.8 7.4 %fusion = f32[256,8,1024]{0,2,1:T(8,128)} fusion(f32[8,4,256,256]{2,3,1,0:T(8,128)} %copy.21, f32[8]{0:T(128)S(1)} %fusion.21, pred[8,1024]{1,0:T(8,128)(4,1)S(1)} %bitcast.65), kind=kLoop, calls=%fused_computation.2 | loop fusion | flops 4194304 | bytes 16785440 | tf_op jit(solution)/shard_map/mul | solution.py:32
  35.3 5.3 %all-to-all-start = ((f32[8,1,256,1024]{2,3,1,0:T(8,128)}), f32[8,1,256,1024]{2,3,1,0:T(8,128)}, u32[]{:S(2)}, u32[]{:S(2)}) async-start(f32[8,1,256,1024]{2,3,1,0:T(8,128)} %bitcast.59), calls=%async_computation | async-start | bytes 16777216 | tf_op jit(solution)/shard_map/all_to_all | solution.py:33
  40.7 0.6 fusion.10
  41.3 0.6 fusion.13
  41.9 0.8 pad_maximum_fusion
  42.8 92.3 %all-to-all-done = f32[8,1,256,1024]{2,3,1,0:T(8,128)} async-done(((f32[8,1,256,1024]{2,3,1,0:T(8,128)}), f32[8,1,256,1024]{2,3,1,0:T(8,128)}, u32[]{:S(2)}, u32[]{:S(2)}) %all-to-all-start) | async-done | bytes 8388640 | tf_op jit(solution)/shard_map/all_to_all | solution.py:33
  135.1 4.1 %bitcast_reduce_fusion = f32[256,1024]{0,1:T(8,128)S(1)} fusion(f32[8,1,256,1024]{2,3,1,0:T(8,128)} %all-to-all-done), kind=kLoop, calls=%fused_computation.3 | loop fusion | flops 1835008 | bytes 9437184 | tf_op jit(solution)/shard_map/reduce_sum | solution.py:34
  139.2 5.1 %fusion.22 = f32[256,512]{1,0:T(8,128)S(1)} fusion(f32[256,1024]{0,1:T(8,128)S(1)} %bitcast_reduce_fusion, f32[1024,512]{0,1:T(8,128)} %all-gather.4.cloned.1.call-done), kind=kOutput, calls=%fused_computation.35 | convolution fusion | flops 1610612736 | bytes 3670016 | tf_op jit(solution)/shard_map/dot_general | solution.py:8
  144.3 1.1 fusion.17
  145.4 0.2 all-reduce.3.cloned.1.call-start
  145.7 0.4 fusion.5
  146.1 1.3 fusion.19
  147.4 0.4 fusion.1
  147.8 1.1 fusion.23
  148.9 0.6 fusion.8
  149.5 0.7 fusion.20
  150.2 23.6 %all-gather.6.cloned.1.call-done = f32[1024,256]{1,0:T(8,128)} async-done(((f32[256,256]{1,0:T(8,128)}), f32[1024,256]{1,0:T(8,128)}) %all-gather.6.cloned.1.call-update) | async-done | bytes 1048592 | tf_op jit(solution)/shard_map/all_gather | solution.py:45
  173.8 1.3 reduce_sum.19
  175.1 0.6 convolution_add_fusion.2
  175.7 39.1 %all-reduce.3.cloned.1.call-done = (f32[256,256]{1,0:T(8,128)}, f32[256,256]{1,0:T(8,128)}) async-done(((f32[256,256]{1,0:T(8,128)}, f32[256,256]{1,0:T(8,128)}), (f32[256,256]{1,0:T(8,128)}, f32[256,256]{1,0:T(8,128)})) %all-reduce.3.cloned.1.call-update) | async-done | bytes 524304 | tf_op jit(solution)/shard_map/psum | solution.py:46
  214.8 1.3 fusion.4
  216.2 2.3 %fusion.3 = f32[1,256,256]{2,1,0:T(8,128)} fusion(f32[256,256]{1,0:T(8,128)} %get-tuple-element.5, f32[256,256]{1,0:T(8,128)S(1)} %fusion.8, f32[256,256]{1,0:T(8,128)S(1)} %fusion.5, f32[256,256]{1,0:T(8,128)S(1)} %fusion.4), kind=kOutput, calls=%fused_computation.8 | convolution fusion | flops 201457664 | bytes 1310720 | tf_op jit(solution)/shard_map/dot_general | solution.py:8
  (23 shorter events, 0.2 us)
Async XLA Ops:
  7.2 33.5 %copy-start = (f32[1,256,256]{2,1,0:T(8,128)S(1)}, f32[1,256,256]{2,1,0:T(8,128)}, u32[]{:S(2)}) copy-start(f32[1,256,256]{2,1,0:T(8,128)} %param.13) | copy-start | bytes 786436
  35.3 5.4 %copy-start.5 = (f32[1,256,256]{2,1,0:T(8,128)S(1)}, f32[1,256,256]{2,1,0:T(8,128)}, u32[]{:S(2)}) copy-start(f32[1,256,256]{2,1,0:T(8,128)} %param.12) | copy-start | bytes 786436
  35.3 6.0 %copy-start.1 = (f32[1,256,256]{2,1,0:T(8,128)S(1)}, f32[1,256,256]{2,1,0:T(8,128)}, u32[]{:S(2)}) copy-start(f32[1,256,256]{2,1,0:T(8,128)} %param.10) | copy-start | bytes 786436
  35.3 6.0 %copy-start.6 = (f32[1,256,256]{2,1,0:T(8,128)S(1)}, f32[1,256,256]{2,1,0:T(8,128)}, u32[]{:S(2)}) copy-start(f32[1,256,256]{2,1,0:T(8,128)} %param.9) | copy-start | bytes 786436
  35.3 99.8 %all-to-all-start = ((f32[8,1,256,1024]{2,3,1,0:T(8,128)}), f32[8,1,256,1024]{2,3,1,0:T(8,128)}, u32[]{:S(2)}, u32[]{:S(2)}) async-start(f32[8,1,256,1024]{2,3,1,0:T(8,128)} %bitcast.59), calls=%async_computation | async-start | bytes 16777216 | tf_op jit(solution)/shard_map/all_to_all | solution.py:33
  40.6 98.6 %all-gather.4.cloned.1.call-start = ((), (), s32[]{:S(2)}) async-start(), calls=%async_computation.1 | async-start | bytes 2621440 | tf_op jit(solution)/shard_map/all_gather | solution.py:35
  41.3 104.4 %copy-start.7 = (f32[1,256,256]{2,1,0:T(8,128)S(1)}, f32[1,256,256]{2,1,0:T(8,128)}, u32[]{:S(2)}) copy-start(f32[1,256,256]{2,1,0:T(8,128)} %param.11) | copy-start | bytes 786436
  42.8 131.0 %all-gather.6.cloned.1.call-start = ((), (), s32[]{:S(2)}) async-start(), calls=%async_computation.2 | async-start | bytes 1310720 | tf_op jit(solution)/shard_map/all_gather | solution.py:45
  145.4 69.4 %all-reduce.3.cloned.1.call-start = ((), (), s32[]{:S(2)}) async-start(), calls=%async_computation.3 | async-start | bytes 1048576 | tf_op jit(solution)/shard_map/psum | solution.py:46
  147.8 70.8 %copy-start.2 = (f32[256,256]{1,0:T(8,128)}, f32[256,256]{1,0:T(8,128)S(1)}, u32[]{:S(2)}) copy-start(f32[256,256]{1,0:T(8,128)S(1)} %fusion.1) | copy-start | bytes 786436
  175.7 42.8 %copy-start.3 = (f32[256,256]{1,0:T(8,128)}, f32[256,256]{1,0:T(8,128)S(1)}, u32[]{:S(2)}) copy-start(f32[256,256]{1,0:T(8,128)S(1)} %convolution_add_fusion.2) | copy-start | bytes 786436
  216.1 2.4 %copy-start.4 = (f32[256,256]{1,0:T(8,128)}, f32[256,256]{1,0:T(8,128)S(1)}, u32[]{:S(2)}) copy-start(f32[256,256]{1,0:T(8,128)S(1)} %fusion.4) | copy-start | bytes 786436
Sparse Core Ops, SparseCore 0:
  43.0 48.5 all-gather.3
  145.6 28.2 all-gather.5
  176.8 37.9 all-reduce.2
